TPU v7x, 256 devices: a whole 4x4x8 slice. The times are simulated.
256 devices in a mesh: pipe: 2 (over core), expert: 16 (over y, x), dp: 8 (over z).
Axes of the slice: x: 4, y: 4, z: 8, core: 2. Of those that a mesh axis runs over, the one named last changes fastest.
Arguments:
- tokens: bfloat16 [2048, 6144], P('expert'), may hold values from -6 to 6
- expert_ids: int32 [2048, 2], P('expert'), may hold values from 0 to 15, all different within a row; in each aligned block of 128 rows (0 to 127, 128 to 255, ...) at most 24 rows name the same one
- w_router: bfloat16 [6144, 16], replicated, may hold values from -0.078125 to 0.078125
- w_gate: bfloat16 [16, 6144, 4096], P('expert', None, ('pipe', 'dp')), may hold values from -0.078125 to 0.078125
- w_up: bfloat16 [16, 6144, 4096], P('expert', None, ('pipe', 'dp')), may hold values from -0.078125 to 0.078125
- w_down: bfloat16 [16, 4096, 6144], P('expert', ('pipe', 'dp')), may hold values from -0.125 to 0.125
Outputs:
- mixed: bfloat16 [2048, 6144], P('expert', ('pipe', 'dp'))
Inputs may be any that keep to these rules, and one draw needn't show every extreme that they name: `expert_ids`: in each aligned block of 128 tokens no expert is named by more than 24 of the block's choices, a bound that some block reaches; the two experts of a token differ.
All inputs are finite; a program needn't handle non-finite values.
Results may differ from a plain program's by a relative error of at most 0.018.
Values may be sent and summed in bfloat16 or wider, within the bound.
A program may use at most 64 MiB of HBM per device.

v0:
```python
import jax
import jax.numpy as jnp
from jax import lax
from jax.sharding import PartitionSpec as P


def slots_of(ids, experts):
    blocks = ids.shape[0]
    flat = ids.reshape(blocks, -1)
    onehot = (flat[:, :, None] == jnp.arange(experts, dtype=jnp.int32)[None, None, :]).astype(
        jnp.int32
    )
    before = jnp.cumsum(onehot, axis=1) - onehot
    slot = jnp.sum(before * onehot, axis=-1)
    return (flat, slot)


def dispatch(x_rows, id_rows, experts, capacity):
    count, width = x_rows.shape
    topk = id_rows.shape[1]
    flat, slot = slots_of(id_rows[None], experts)
    dest = flat[0] * capacity + slot[0]
    select = (jnp.arange(experts * capacity, dtype=jnp.int32)[:, None] == dest[None, :]).astype(
        jnp.bfloat16
    )
    repeated = jnp.repeat(x_rows, topk, axis=0)
    placed = jnp.dot(select, repeated, preferred_element_type=jnp.float32).astype(jnp.bfloat16)
    return (placed.reshape(experts, capacity, width), dest)


def body(tokens, expert_ids, w_router, w_gate, w_up, w_down):
    count, width = tokens.shape
    topk = expert_ids.shape[1]
    experts = lax.axis_size("expert") * w_gate.shape[0]
    capacity = 3 * count * topk // (2 * experts)
    groups = lax.axis_size(("pipe", "dp"))
    columns = width // groups
    start = lax.axis_index(("pipe", "dp")) * columns
    mine = lax.dynamic_slice_in_dim(tokens, start, columns, 1)
    local, dest = dispatch(mine, expert_ids, experts, capacity)
    arrived = lax.all_to_all(local, "expert", split_axis=0, concat_axis=0, tiled=True)
    arrived = arrived.reshape(experts * capacity, columns)
    inputs = lax.all_gather(arrived, ("pipe", "dp"), axis=1, tiled=True)
    gate = jnp.dot(inputs, w_gate[0], preferred_element_type=jnp.float32)
    upper = jnp.dot(inputs, w_up[0], preferred_element_type=jnp.float32)
    hidden = (jax.nn.silu(gate) * upper).astype(jnp.bfloat16)
    term = jnp.dot(hidden, w_down[0], preferred_element_type=jnp.float32).astype(jnp.bfloat16)
    logits = jnp.dot(tokens, w_router, preferred_element_type=jnp.float32)
    chosen = jnp.take_along_axis(logits, expert_ids, axis=1)
    first = jax.nn.sigmoid(chosen[:, 0] - chosen[:, 1])
    gates = jnp.stack([first, 1.0 - first], axis=1)
    summed = lax.psum_scatter(term, ("pipe", "dp"), scatter_dimension=1, tiled=True)
    returned = lax.all_to_all(
        summed.reshape(experts, capacity, columns),
        "expert",
        split_axis=0,
        concat_axis=0,
        tiled=True,
    )
    picked = jnp.take(returned.reshape(experts * capacity, columns), dest, axis=0)
    picked = picked.reshape(count, topk, columns).astype(jnp.float32)
    return jnp.sum(gates[:, :, None] * picked, axis=1).astype(jnp.bfloat16)


def solution(mesh):
    placed = (
        P("expert", None),
        P("expert", None),
        P(),
        P("expert", None, ("pipe", "dp")),
        P("expert", None, ("pipe", "dp")),
        P("expert", ("pipe", "dp"), None),
    )
    return jax.shard_map(
        body, mesh=mesh, in_specs=placed, out_specs=P("expert", ("pipe", "dp")), check_vma=False
    )
```

profile of v0, /device:TPU:1, one launch (start us, length us, event | category | flops | bytes accessed | tf_op | source)
XLA Modules:
  0.0 195.6 jit_solution(6473342927977986380)
XLA Ops:
  6.5 0.9 copy.45
  7.5 0.1 eq.40
  7.7 0.6 reduce-window.6
  8.2 0.8 slice_reduce_fusion
  9.0 0.9 constant_dynamic-slice_fusion
  10.1 0.7 reduce-window.9
  11.0 0.7 fusion.20
  11.8 0.6 copy-done.3
  12.3 0.7 multiply_add_fusion
  13.0 0.3 convolution_convert_fusion.1
  13.3 15.7 %all_to_all.10 = bf16[16,24,384]{2,1,0:T(8,128)(2,1)} all-to-all(bf16[16,24,384]{2,1,0:T(8,128)(2,1)S(1)} %bitcast.50), channel_id=1, replica_groups=mesh['pipe'=2,'expert'=16,'dp'=8] {'expert'}, dimensions={0} | all-to-all | bytes 589824 | tf_op jit(solution)/shard_map/all_to_all | solution.py:41
  29.0 43.7 %all-gather.2.cloned.1.call-done = bf16[384,6144]{1,0:T(8,128)(2,1)} async-done(((bf16[384,384]{1,0:T(8,128)(2,1)}), bf16[384,6144]{1,0:T(8,128)(2,1)}) %all-gather.2.cloned.1.call-update) | async-done | bytes 4718608 | tf_op jit(solution)/shard_map/all_gather | solution.py:43
  72.8 4.7 %fusion.3 = f32[384,256]{1,0:T(8,128)S(1)} fusion(bf16[384,6144]{1,0:T(8,128)(2,1)} %all-gather.2.cloned.1.call-done, bf16[1,6144,256]{2,1,0:T(8,128)(2,1)} %param.9), kind=kOutput, calls=%fused_computation.6 | convolution fusion | flops 1207959552 | bytes 8257536 | tf_op jit(solution)/shard_map/dot_general | solution.py:44
  77.5 10.6 %convolution_convert_fusion = bf16[384,6144]{1,0:T(8,128)(2,1)} fusion(bf16[1,256,6144]{2,1,0:T(8,128)(2,1)S(1)} %copy-done, bf16[384,6144]{1,0:T(8,128)(2,1)} %all-gather.2.cloned.1.call-done, bf16[1,6144,256]{2,1,0:T(8,128)(2,1)} %param.10, f32[384,256]{1,0:T(8,128)S(1)} %fusion.3), kind=kOutput, calls=%fused_computation.2 | convolution fusion | flops 2418868224 | bytes 16121856 | tf_op jit(solution)/shard_map/dot_general | solution.py:47
  88.0 6.6 %copy.52 = bf16[384,6144]{0,1:T(8,128)(2,1)} copy(bf16[384,6144]{1,0:T(8,128)(2,1)} %convolution_convert_fusion) | data formatting | bytes 9437184
  94.7 0.6 copy-done.4
  95.3 0.1 reduce_sum.23
  95.5 0.1 copy.51
  95.6 0.1 mul.61
  95.8 0.1 copy.50
  96.0 0.1 copy.42
  96.1 0.1 reshape.211
  96.3 1.9 fusion.22
  98.2 2.0 %gather_fusion.1 = f32[256]{0:T(256)S(1)} fusion(f32[128,16]{0,1:T(8,128)S(1)} %fusion.22, s32[256]{0:T(256)S(1)} %reshape.211), kind=kCustom, calls=%fused_computation.1 | custom fusion | bytes 4096 | tf_op jit(solution)/shard_map/jit(take_along_axis)/gather | solution.py:49
  100.2 0.1 reshape.214
  100.5 67.4 %reduce-scatter.4.cloned.1.call-done = bf16[384,384]{1,0:T(8,128)(2,1)} async-done(((bf16[6144,384]{1,0:T(8,128)(2,1)}), bf16[384,384]{1,0:T(8,128)(2,1)}) %reduce-scatter.4.cloned.1.call-update) | async-done | bytes 294928
  168.0 1.8 copy.53
  169.8 6.3 %all-to-all-start.1 = ((bf16[16,24,384]{2,1,0:T(8,128)(2,1)}), bf16[16,24,384]{2,1,0:T(8,128)(2,1)S(1)}, u32[]{:S(2)}, u32[]{:S(2)}) async-start(bf16[16,24,384]{2,1,0:T(8,128)(2,1)} %bitcast.49), calls=%async_computation.1 | async-start | bytes 589824 | tf_op jit(solution)/shard_map/all_to_all | solution.py:53
  176.2 8.5 %all-to-all-done.1 = bf16[16,24,384]{2,1,0:T(8,128)(2,1)S(1)} async-done(((bf16[16,24,384]{2,1,0:T(8,128)(2,1)}), bf16[16,24,384]{2,1,0:T(8,128)(2,1)S(1)}, u32[]{:S(2)}, u32[]{:S(2)}) %all-to-all-start.1) | async-done | bytes 294944 | tf_op jit(solution)/shard_map/all_to_all | solution.py:53
  184.6 1.8 gather_fusion
  186.5 1.0 gather.12
  187.5 1.3 multiply_reduce_fusion
  (33 shorter events, 0.8 us)
Async XLA Ops:
  6.5 70.9 %copy-start = (bf16[1,256,6144]{2,1,0:T(8,128)(2,1)S(1)}, bf16[1,256,6144]{2,1,0:T(8,128)(2,1)}, u32[]{:S(2)}) copy-start(bf16[1,256,6144]{2,1,0:T(8,128)(2,1)} %param.11) | copy-start | bytes 9437188
  6.5 66.2 %all-gather.2.cloned.1.call-start = ((), (), s32[]{:S(2)}) async-start(), calls=%async_computation.3 | async-start | bytes 5013504 | tf_op jit(solution)/shard_map/all_gather | solution.py:43
  7.6 1.4 copy-start.5
  11.8 0.6 copy-start.3
  29.0 139.0 %reduce-scatter.4.cloned.1.call-start = ((), (), s32[]{:S(2)}) async-start(), calls=%async_computation.4 | async-start | bytes 5013504
  94.7 0.7 copy-start.4
  94.7 0.8 copy-start.2
  94.7 1.6 copy-start.1
  169.8 14.8 %all-to-all-start.1 = ((bf16[16,24,384]{2,1,0:T(8,128)(2,1)}), bf16[16,24,384]{2,1,0:T(8,128)(2,1)S(1)}, u32[]{:S(2)}, u32[]{:S(2)}) async-start(bf16[16,24,384]{2,1,0:T(8,128)(2,1)} %bitcast.49), calls=%async_computation.1 | async-start | bytes 589824 | tf_op jit(solution)/shard_map/all_to_all | solution.py:53
Sparse Core Ops, SparseCore 0:
  29.1 43.6 all-gather.1
  94.8 73.1 reduce-scatter.3
where the time goes:
time: 196 us
  waiting for transfers between devices  120 us (61%)
  local copies, waits for them, and re-layouts  18.7 us (10%)
  matrix products  17.4 us (9%)
  blocking collectives  15.7 us (8%)
  between operations  13.6 us (7%)
  starting transfers between devices  6.36 us (3%)
  other arithmetic  4.13 us (2%)
    unnamed x3, waiting for transfers between devices  67.5 us
    all_gather x1, waiting for transfers between devices, body(): inputs = lax.all_gather(arrived, ('pipe', 'dp'), axis=1, tiled=True)  43.7 us
    all_to_all x1, blocking collectives, body(): lax.all_to_all(local, 'expert', split_axis=0, concat_axis=0, tiled=True)  15.7 us
    unnamed x15, local copies, waits for them, and re-layouts  10.6 us
    dot_general x1, matrix products, body(): jnp.dot(hidden, w_down[0], preferred_element_type=jnp.float32)  10.6 us
    all_to_all x1, waiting for transfers between devices, body(): lax.all_to_all(summed.reshape(experts, capacity, columns), 'expert', spli...  8.47 us
    all_to_all x1, starting transfers between devices, body(): lax.all_to_all(summed.reshape(experts, capacity, columns), 'expert', spli...  6.32 us
    dot_general x1, matrix products, body(): gate = jnp.dot(inputs, w_gate[0], preferred_element_type=jnp.float32)  4.71 us
  transfers between devices with their start and end apart: 3, of which 3 were waited for; matrix products, arithmetic and copies ran while one was open for 3% of the time, Pallas kernels for 0%

commit v1 on v0

--- a/solution.py
+++ b/solution.py
@@ -40,7 +40,28 @@
     local, dest = dispatch(mine, expert_ids, experts, capacity)
     arrived = lax.all_to_all(local, "expert", split_axis=0, concat_axis=0, tiled=True)
     arrived = arrived.reshape(experts * capacity, columns)
-    inputs = lax.all_gather(arrived, ("pipe", "dp"), axis=1, tiled=True)
+    length, index, rows = (
+        lax.axis_size(("pipe", "dp")),
+        lax.axis_index(("pipe", "dp")),
+        arrived.shape[1],
+    )
+    forward = [(i, (i + 1) % length) for i in range(length)]
+    left = [(i, (i - 1) % length) for i in range(length)]
+    result = jnp.zeros((*arrived.shape[:1], length * rows, *arrived.shape[1 + 1 :]), arrived.dtype)
+    result = lax.dynamic_update_slice_in_dim(result, arrived, index * rows, axis=1)
+    from_left = from_right = arrived
+    half = length // 2
+    for hop in range(1, half + 1):
+        from_left = lax.ppermute(from_left, ("pipe", "dp"), forward)
+        result = lax.dynamic_update_slice_in_dim(
+            result, from_left, (index - hop) % length * rows, axis=1
+        )
+        if hop < length - half:
+            from_right = lax.ppermute(from_right, ("pipe", "dp"), left)
+            result = lax.dynamic_update_slice_in_dim(
+                result, from_right, (index + hop) % length * rows, axis=1
+            )
+    inputs = result
     gate = jnp.dot(inputs, w_gate[0], preferred_element_type=jnp.float32)
     upper = jnp.dot(inputs, w_up[0], preferred_element_type=jnp.float32)
     hidden = (jax.nn.silu(gate) * upper).astype(jnp.bfloat16)

time: 196 us -> 227 us (1.16)
  starting transfers between devices: 6.36 us -> 36.3 us
  local copies, waits for them, and re-layouts: 18.7 us -> 27.1 us
  waiting for transfers between devices: 120 us -> 116 us
  matrix products: 17.4 us -> 14.1 us
    all_gather x1 -> x0, waiting for transfers between devices: 43.7 us -> none  [body(): inputs = lax.all_gather(arrived, ('pipe', 'dp'), axis=1, tiled=True)]
    ppermute x0 -> x15, waiting for transfers between devices: none -> 42.7 us  [the longest x7 24.7 us: body(): from_right = lax.ppermute(from_right, ('pipe', 'dp'), left)]
    ppermute x0 -> x15, starting transfers between devices: none -> 29.7 us  [the longest x7 27.8 us: body(): from_right = lax.ppermute(from_right, ('pipe', 'dp'), left)]
    dynamic_update_slice x0 -> x16, local copies, waits for them, and re-layouts: none -> 4.87 us  [the longest x8 2.43 us: body(): lax.dynamic_update_slice_in_dim(result, from_left, (index - hop) % length...]
    dot_general x1, matrix products: 4.71 us -> 1.42 us  [body(): upper = jnp.dot(inputs, w_up[0], preferred_element_type=jnp.float32)]
    unnamed x15 -> x27, local copies, waits for them, and re-layouts: 10.6 us -> 13.6 us
    unnamed x3 -> x2, waiting for transfers between devices: 67.5 us -> 64.6 us
  transfers between devices with their start and end apart: 3 -> 17, of which waited for: 3 -> 15; matrix products, arithmetic and copies ran while one was open for 3% -> 5% of each run, Pallas kernels for 0% -> 0%
where the time goes in v1:
time: 227 us
  waiting for transfers between devices  116 us (51%)
  starting transfers between devices  36.3 us (16%)
  local copies, waits for them, and re-layouts  27.1 us (12%)
  blocking collectives  15.5 us (7%)
  matrix products  14.1 us (6%)
  between operations  13.8 us (6%)
  other arithmetic  4.1 us (2%)
    unnamed x2, waiting for transfers between devices  64.6 us
    ppermute x7, starting transfers between devices, body(): from_right = lax.ppermute(from_right, ('pipe', 'dp'), left)  27.8 us
    ppermute x7, waiting for transfers between devices, body(): from_right = lax.ppermute(from_right, ('pipe', 'dp'), left)  24.7 us
    ppermute x8, waiting for transfers between devices, body(): from_left = lax.ppermute(from_left, ('pipe', 'dp'), forward)  18.1 us
    all_to_all x1, blocking collectives, body(): lax.all_to_all(local, 'expert', split_axis=0, concat_axis=0, tiled=True)  15.5 us
    unnamed x27, local copies, waits for them, and re-layouts  13.6 us
    dot_general x1, matrix products, body(): jnp.dot(hidden, w_down[0], preferred_element_type=jnp.float32)  10.5 us
    all_to_all x1, waiting for transfers between devices, body(): lax.all_to_all(summed.reshape(experts, capacity, columns), 'expert', spli...  8.39 us
  transfers between devices with their start and end apart: 17, of which 15 were waited for; matrix products, arithmetic and copies ran while one was open for 5% of the time, Pallas kernels for 0%

profile of v1, /device:TPU:1, one launch (start us, length us, event | category | flops | bytes accessed | tf_op | source)
XLA Modules:
  0.0 226.8 jit_solution(17767299399627187138)
XLA Ops:
  13.3 15.5 %all_to_all.10 = bf16[16,24,384]{2,1,0:T(8,128)(2,1)S(1)} all-to-all(bf16[16,24,384]{2,1,0:T(8,128)(2,1)S(1)} %bitcast.50), channel_id=1, replica_groups=mesh['pipe'=2,'expert'=16,'dp'=8] {'expert'}, dimensions={0} | all-to-all | bytes 589824 | tf_op jit(solution)/shard_map/all_to_all | solution.py:41
  28.8 1.6 collective-permute-start
  30.4 5.6 %collective-permute-start.1 = (bf16[384,384]{1,0:T(8,128)(2,1)S(1)}, bf16[384,384]{1,0:T(8,128)(2,1)S(1)}, u32[]{:S(2)}, u32[]{:S(2)}) collective-permute-start(bf16[384,384]{1,0:T(8,128)(2,1)S(1)} %bitcast.48), channel_id=1, source_target_pairs={{0,135},{1,0},{2,1},{3,2},{4,3},{5,4},{6,5},{7,6},{128,7},{129,128... | collective-permute-start | bytes 884744 | tf_op jit(solution)/shard_map/ppermute | solution.py:60
  36.1 5.6 %collective-permute-done = bf16[384,384]{1,0:T(8,128)(2,1)S(1)} collective-permute-done((bf16[384,384]{1,0:T(8,128)(2,1)S(1)}, bf16[384,384]{1,0:T(8,128)(2,1)S(1)}, u32[]{:S(2)}, u32[]{:S(2)}) %collective-permute-start) | collective-permute-done | bytes 294944 | tf_op jit(solution)/shard_map/ppermute | solution.py:55
  42.5 3.7 %collective-permute-start.3 = (bf16[384,384]{1,0:T(8,128)(2,1)S(1)}, bf16[384,384]{1,0:T(8,128)(2,1)}, u32[]{:S(2)}, u32[]{:S(2)}) collective-permute-start(bf16[384,384]{1,0:T(8,128)(2,1)S(1)} %collective-permute-done.1), channel_id=1, source_target_pairs={{0,135},{1,0},{2,1},{3,2},{4,3},{5,4},{6,5},{7,6},{128,7},{129,128... | collective-permute-start | bytes 884744 | tf_op jit(solution)/shard_map/ppermute | solution.py:60
  46.2 4.1 %collective-permute-done.2 = bf16[384,384]{1,0:T(8,128)(2,1)} collective-permute-done((bf16[384,384]{1,0:T(8,128)(2,1)S(1)}, bf16[384,384]{1,0:T(8,128)(2,1)}, u32[]{:S(2)}, u32[]{:S(2)}) %collective-permute-start.2) | collective-permute-done | bytes 294944 | tf_op jit(solution)/shard_map/ppermute | solution.py:55
  50.3 1.9 collective-permute-done.3
  52.2 3.8 %collective-permute-start.5 = (bf16[384,384]{1,0:T(8,128)(2,1)}, bf16[384,384]{1,0:T(8,128)(2,1)}, u32[]{:S(2)}, u32[]{:S(2)}) collective-permute-start(bf16[384,384]{1,0:T(8,128)(2,1)} %collective-permute-done.3), channel_id=1, source_target_pairs={{0,135},{1,0},{2,1},{3,2},{4,3},{5,4},{6,5},{7,6},{128,7},{129,128... | collective-permute-start | bytes 884744 | tf_op jit(solution)/shard_map/ppermute | solution.py:60
  56.0 3.1 %collective-permute-done.4 = bf16[384,384]{1,0:T(8,128)(2,1)} collective-permute-done((bf16[384,384]{1,0:T(8,128)(2,1)}, bf16[384,384]{1,0:T(8,128)(2,1)}, u32[]{:S(2)}, u32[]{:S(2)}) %collective-permute-start.4) | collective-permute-done | bytes 294944 | tf_op jit(solution)/shard_map/ppermute | solution.py:55
  59.8 2.7 %collective-permute-done.5 = bf16[384,384]{1,0:T(8,128)(2,1)} collective-permute-done((bf16[384,384]{1,0:T(8,128)(2,1)}, bf16[384,384]{1,0:T(8,128)(2,1)}, u32[]{:S(2)}, u32[]{:S(2)}) %collective-permute-start.5) | collective-permute-done | bytes 294944 | tf_op jit(solution)/shard_map/ppermute | solution.py:60
  62.6 3.7 %collective-permute-start.7 = (bf16[384,384]{1,0:T(8,128)(2,1)}, bf16[384,384]{1,0:T(8,128)(2,1)S(1)}, u32[]{:S(2)}, u32[]{:S(2)}) collective-permute-start(bf16[384,384]{1,0:T(8,128)(2,1)} %collective-permute-done.5), channel_id=1, source_target_pairs={{0,135},{1,0},{2,1},{3,2},{4,3},{5,4},{6,5},{7,6},{128,7},{129,128... | collective-permute-start | bytes 884744 | tf_op jit(solution)/shard_map/ppermute | solution.py:60
  66.3 1.5 collective-permute-done.6
  70.0 3.2 %collective-permute-done.7 = bf16[384,384]{1,0:T(8,128)(2,1)S(1)} collective-permute-done((bf16[384,384]{1,0:T(8,128)(2,1)}, bf16[384,384]{1,0:T(8,128)(2,1)S(1)}, u32[]{:S(2)}, u32[]{:S(2)}) %collective-permute-start.7) | collective-permute-done | bytes 294944 | tf_op jit(solution)/shard_map/ppermute | solution.py:60
  73.1 3.6 %collective-permute-start.9 = (bf16[384,384]{1,0:T(8,128)(2,1)S(1)}, bf16[384,384]{1,0:T(8,128)(2,1)S(1)}, u32[]{:S(2)}, u32[]{:S(2)}) collective-permute-start(bf16[384,384]{1,0:T(8,128)(2,1)S(1)} %collective-permute-done.7), channel_id=1, source_target_pairs={{0,135},{1,0},{2,1},{3,2},{4,3},{5,4},{6,5},{7,6},{128,7},{129,128... | collective-permute-start | bytes 884744 | tf_op jit(solution)/shard_map/ppermute | solution.py:60
  79.0 4.5 %collective-permute-done.9 = bf16[384,384]{1,0:T(8,128)(2,1)S(1)} collective-permute-done((bf16[384,384]{1,0:T(8,128)(2,1)S(1)}, bf16[384,384]{1,0:T(8,128)(2,1)S(1)}, u32[]{:S(2)}, u32[]{:S(2)}) %collective-permute-start.9) | collective-permute-done | bytes 294944 | tf_op jit(solution)/shard_map/ppermute | solution.py:60
  83.5 3.7 %collective-permute-start.11 = (bf16[384,384]{1,0:T(8,128)(2,1)S(1)}, bf16[384,384]{1,0:T(8,128)(2,1)S(1)}, u32[]{:S(2)}, u32[]{:S(2)}) collective-permute-start(bf16[384,384]{1,0:T(8,128)(2,1)S(1)} %collective-permute-done.9), channel_id=1, source_target_pairs={{0,135},{1,0},{2,1},{3,2},{4,3},{5,4},{6,5},{7,6},{128,7},{129,128... | collective-permute-start | bytes 884744 | tf_op jit(solution)/shard_map/ppermute | solution.py:60
  87.7 6.0 %collective-permute-done.11 = bf16[384,384]{1,0:T(8,128)(2,1)S(1)} collective-permute-done((bf16[384,384]{1,0:T(8,128)(2,1)S(1)}, bf16[384,384]{1,0:T(8,128)(2,1)S(1)}, u32[]{:S(2)}, u32[]{:S(2)}) %collective-permute-start.11) | collective-permute-done | bytes 294944 | tf_op jit(solution)/shard_map/ppermute | solution.py:60
  93.7 3.7 %collective-permute-start.13 = (bf16[384,384]{1,0:T(8,128)(2,1)S(1)}, bf16[384,384]{1,0:T(8,128)(2,1)S(1)}, u32[]{:S(2)}, u32[]{:S(2)}) collective-permute-start(bf16[384,384]{1,0:T(8,128)(2,1)S(1)} %collective-permute-done.11), channel_id=1, source_target_pairs={{0,135},{1,0},{2,1},{3,2},{4,3},{5,4},{6,5},{7,6},{128,7},{129,128... | collective-permute-start | bytes 884744 | tf_op jit(solution)/shard_map/ppermute | solution.py:60
  97.8 6.2 %collective-permute-done.13 = bf16[384,384]{1,0:T(8,128)(2,1)S(1)} collective-permute-done((bf16[384,384]{1,0:T(8,128)(2,1)S(1)}, bf16[384,384]{1,0:T(8,128)(2,1)S(1)}, u32[]{:S(2)}, u32[]{:S(2)}) %collective-permute-start.13) | collective-permute-done | bytes 294944 | tf_op jit(solution)/shard_map/ppermute | solution.py:60
  104.0 3.5 %collective-permute-done.14 = bf16[384,384]{1,0:T(8,128)(2,1)S(1)} collective-permute-done((bf16[384,384]{1,0:T(8,128)(2,1)S(1)}, bf16[384,384]{1,0:T(8,128)(2,1)S(1)}, u32[]{:S(2)}, u32[]{:S(2)}) %collective-permute-start.14) | collective-permute-done | bytes 294944 | tf_op jit(solution)/shard_map/ppermute | solution.py:55
  107.6 2.2 copy-done.1
  109.8 1.4 fusion.1
  111.2 10.5 %convolution_convert_fusion = bf16[384,6144]{1,0:T(8,128)(2,1)} fusion(bf16[1,256,6144]{2,1,0:T(8,128)(2,1)S(1)} %copy-done, f32[384,256]{1,0:T(8,128)S(1)} %fusion.1, bf16[384,6144]{1,0:T(8,128)(2,1)} %copy-done.1, bf16[1,6144,256]{2,1,0:T(8,128)(2,1)} %param.9), kind=kOutput, calls=%fused_computation.2 | convolution fusion | flops 2418868224 | bytes 16121856 | tf_op jit(solution)/shard_map/dot_general | solution.py:68
  121.8 6.7 %copy.52 = bf16[384,6144]{0,1:T(8,128)(2,1)} copy(bf16[384,6144]{1,0:T(8,128)(2,1)} %convolution_convert_fusion) | data formatting | bytes 9437184
  130.1 1.9 fusion.13
  132.0 2.0 gather_fusion.1
  134.4 64.6 %reduce-scatter.4.cloned.1.call-done = bf16[384,384]{1,0:T(8,128)(2,1)} async-done(((bf16[6144,384]{1,0:T(8,128)(2,1)}), bf16[384,384]{1,0:T(8,128)(2,1)}) %reduce-scatter.4.cloned.1.call-update) | async-done | bytes 294928
  198.9 1.8 copy.53
  200.8 6.6 %all-to-all-start.1 = ((bf16[16,24,384]{2,1,0:T(8,128)(2,1)}), bf16[16,24,384]{2,1,0:T(8,128)(2,1)S(1)}, u32[]{:S(2)}, u32[]{:S(2)}) async-start(bf16[16,24,384]{2,1,0:T(8,128)(2,1)} %bitcast.46), calls=%async_computation.1 | async-start | bytes 589824 | tf_op jit(solution)/shard_map/all_to_all | solution.py:74
  207.4 8.4 %all-to-all-done.1 = bf16[16,24,384]{2,1,0:T(8,128)(2,1)S(1)} async-done(((bf16[16,24,384]{2,1,0:T(8,128)(2,1)}), bf16[16,24,384]{2,1,0:T(8,128)(2,1)S(1)}, u32[]{:S(2)}, u32[]{:S(2)}) %all-to-all-start.1) | async-done | bytes 294944 | tf_op jit(solution)/shard_map/all_to_all | solution.py:74
  215.8 1.8 gather_fusion
  218.6 1.3 multiply_reduce_fusion
  (89 shorter events, 16.4 us)
Async XLA Ops:
  6.5 104.7 %copy-start = (bf16[1,256,6144]{2,1,0:T(8,128)(2,1)S(1)}, bf16[1,256,6144]{2,1,0:T(8,128)(2,1)}, u32[]{:S(2)}) copy-start(bf16[1,256,6144]{2,1,0:T(8,128)(2,1)} %param.11) | copy-start | bytes 9437188
  6.5 192.4 %reduce-scatter.4.cloned.1.call-start = ((), (), s32[]{:S(2)}) async-start(), calls=%async_computation.3 | async-start | bytes 5013504
  7.6 1.4 copy-start.10
  11.7 0.6 copy-start.8
  28.8 12.8 %collective-permute-start = (bf16[384,384]{1,0:T(8,128)(2,1)S(1)}, bf16[384,384]{1,0:T(8,128)(2,1)S(1)}, u32[]{:S(2)}, u32[]{:S(2)}) collective-permute-start(bf16[384,384]{1,0:T(8,128)(2,1)S(1)} %bitcast.47), channel_id=1, source_target_pairs={{0,1},{1,2},{2,3},{3,4},{4,5},{5,6},{6,7},{7,128},{128,129},{129,1... | collective-permute-start | bytes 884744 | tf_op jit(solution)/shard_map/ppermute | solution.py:55
  30.4 11.3 %collective-permute-start.1 = (bf16[384,384]{1,0:T(8,128)(2,1)S(1)}, bf16[384,384]{1,0:T(8,128)(2,1)S(1)}, u32[]{:S(2)}, u32[]{:S(2)}) collective-permute-start(bf16[384,384]{1,0:T(8,128)(2,1)S(1)} %bitcast.48), channel_id=1, source_target_pairs={{0,135},{1,0},{2,1},{3,2},{4,3},{5,4},{6,5},{7,6},{128,7},{129,128... | collective-permute-start | bytes 884744 | tf_op jit(solution)/shard_map/ppermute | solution.py:60
  41.6 10.5 %copy-start.4 = (bf16[384,384]{1,0:T(8,128)(2,1)}, bf16[384,384]{1,0:T(8,128)(2,1)S(1)}, u32[]{:S(2)}) copy-start(bf16[384,384]{1,0:T(8,128)(2,1)S(1)} %collective-permute-done) | copy-start | bytes 884740
  41.6 8.6 %collective-permute-start.2 = (bf16[384,384]{1,0:T(8,128)(2,1)S(1)}, bf16[384,384]{1,0:T(8,128)(2,1)}, u32[]{:S(2)}, u32[]{:S(2)}) collective-permute-start(bf16[384,384]{1,0:T(8,128)(2,1)S(1)} %collective-permute-done), channel_id=1, source_target_pairs={{0,1},{1,2},{2,3},{3,4},{4,5},{5,6},{6,7},{7,128},{128,129},{129,1... | collective-permute-start | bytes 884744 | tf_op jit(solution)/shard_map/ppermute | solution.py:55
  41.8 0.7 copy-start.2
  42.5 9.7 %collective-permute-start.3 = (bf16[384,384]{1,0:T(8,128)(2,1)S(1)}, bf16[384,384]{1,0:T(8,128)(2,1)}, u32[]{:S(2)}, u32[]{:S(2)}) collective-permute-start(bf16[384,384]{1,0:T(8,128)(2,1)S(1)} %collective-permute-done.1), channel_id=1, source_target_pairs={{0,135},{1,0},{2,1},{3,2},{4,3},{5,4},{6,5},{7,6},{128,7},{129,128... | collective-permute-start | bytes 884744 | tf_op jit(solution)/shard_map/ppermute | solution.py:60
  50.3 8.8 %collective-permute-start.4 = (bf16[384,384]{1,0:T(8,128)(2,1)}, bf16[384,384]{1,0:T(8,128)(2,1)}, u32[]{:S(2)}, u32[]{:S(2)}) collective-permute-start(bf16[384,384]{1,0:T(8,128)(2,1)} %collective-permute-done.2), channel_id=1, source_target_pairs={{0,1},{1,2},{2,3},{3,4},{4,5},{5,6},{6,7},{7,128},{128,129},{129,1... | collective-permute-start | bytes 884744 | tf_op jit(solution)/shard_map/ppermute | solution.py:55
  52.2 10.4 %collective-permute-start.5 = (bf16[384,384]{1,0:T(8,128)(2,1)}, bf16[384,384]{1,0:T(8,128)(2,1)}, u32[]{:S(2)}, u32[]{:S(2)}) collective-permute-start(bf16[384,384]{1,0:T(8,128)(2,1)} %collective-permute-done.3), channel_id=1, source_target_pairs={{0,135},{1,0},{2,1},{3,2},{4,3},{5,4},{6,5},{7,6},{128,7},{129,128... | collective-permute-start | bytes 884744 | tf_op jit(solution)/shard_map/ppermute | solution.py:60
  56.0 3.8 %copy-start.5 = (bf16[384,384]{1,0:T(8,128)(2,1)S(1)}, bf16[384,384]{1,0:T(8,128)(2,1)}, u32[]{:S(2)}) copy-start(bf16[384,384]{1,0:T(8,128)(2,1)} %copy-done.4) | copy-start | bytes 884740
  56.0 10.3 %copy-start.3 = (bf16[384,384]{1,0:T(8,128)(2,1)S(1)}, bf16[384,384]{1,0:T(8,128)(2,1)}, u32[]{:S(2)}) copy-start(bf16[384,384]{1,0:T(8,128)(2,1)} %copy-done.2) | copy-start | bytes 884740
  59.1 8.7 %collective-permute-start.6 = (bf16[384,384]{1,0:T(8,128)(2,1)}, bf16[384,384]{1,0:T(8,128)(2,1)S(1)}, u32[]{:S(2)}, u32[]{:S(2)}) collective-permute-start(bf16[384,384]{1,0:T(8,128)(2,1)} %collective-permute-done.4), channel_id=1, source_target_pairs={{0,1},{1,2},{2,3},{3,4},{4,5},{5,6},{6,7},{7,128},{128,129},{129,1... | collective-permute-start | bytes 884744 | tf_op jit(solution)/shard_map/ppermute | solution.py:55
  59.7 50.1 %copy-start.11 = (bf16[1,6144,256]{2,1,0:T(8,128)(2,1)S(1)}, bf16[1,6144,256]{2,1,0:T(8,128)(2,1)}, u32[]{:S(2)}) copy-start(bf16[1,6144,256]{2,1,0:T(8,128)(2,1)} %param.10) | copy-start | bytes 9437188
  62.6 10.6 %collective-permute-start.7 = (bf16[384,384]{1,0:T(8,128)(2,1)}, bf16[384,384]{1,0:T(8,128)(2,1)S(1)}, u32[]{:S(2)}, u32[]{:S(2)}) collective-permute-start(bf16[384,384]{1,0:T(8,128)(2,1)} %collective-permute-done.5), channel_id=1, source_target_pairs={{0,135},{1,0},{2,1},{3,2},{4,3},{5,4},{6,5},{7,6},{128,7},{129,128... | collective-permute-start | bytes 884744 | tf_op jit(solution)/shard_map/ppermute | solution.py:60
  67.8 9.9 %collective-permute-start.8 = (bf16[384,384]{1,0:T(8,128)(2,1)S(1)}, bf16[384,384]{1,0:T(8,128)(2,1)S(1)}, u32[]{:S(2)}, u32[]{:S(2)}) collective-permute-start(bf16[384,384]{1,0:T(8,128)(2,1)S(1)} %collective-permute-done.6), channel_id=1, source_target_pairs={{0,1},{1,2},{2,3},{3,4},{4,5},{5,6},{6,7},{7,128},{128,129},{129,1... | collective-permute-start | bytes 884744 | tf_op jit(solution)/shard_map/ppermute | solution.py:55
  73.1 10.4 %collective-permute-start.9 = (bf16[384,384]{1,0:T(8,128)(2,1)S(1)}, bf16[384,384]{1,0:T(8,128)(2,1)S(1)}, u32[]{:S(2)}, u32[]{:S(2)}) collective-permute-start(bf16[384,384]{1,0:T(8,128)(2,1)S(1)} %collective-permute-done.7), channel_id=1, source_target_pairs={{0,135},{1,0},{2,1},{3,2},{4,3},{5,4},{6,5},{7,6},{128,7},{129,128... | collective-permute-start | bytes 884744 | tf_op jit(solution)/shard_map/ppermute | solution.py:60
  77.8 9.8 %collective-permute-start.10 = (bf16[384,384]{1,0:T(8,128)(2,1)S(1)}, bf16[384,384]{1,0:T(8,128)(2,1)S(1)}, u32[]{:S(2)}, u32[]{:S(2)}) collective-permute-start(bf16[384,384]{1,0:T(8,128)(2,1)S(1)} %collective-permute-done.8), channel_id=1, source_target_pairs={{0,1},{1,2},{2,3},{3,4},{4,5},{5,6},{6,7},{7,128},{128,129},{129,1... | collective-permute-start | bytes 884744 | tf_op jit(solution)/shard_map/ppermute | solution.py:55
  83.5 10.2 %collective-permute-start.11 = (bf16[384,384]{1,0:T(8,128)(2,1)S(1)}, bf16[384,384]{1,0:T(8,128)(2,1)S(1)}, u32[]{:S(2)}, u32[]{:S(2)}) collective-permute-start(bf16[384,384]{1,0:T(8,128)(2,1)S(1)} %collective-permute-done.9), channel_id=1, source_target_pairs={{0,135},{1,0},{2,1},{3,2},{4,3},{5,4},{6,5},{7,6},{128,7},{129,128... | collective-permute-start | bytes 884744 | tf_op jit(solution)/shard_map/ppermute | solution.py:60
  87.5 10.0 %collective-permute-start.12 = (bf16[384,384]{1,0:T(8,128)(2,1)S(1)}, bf16[384,384]{1,0:T(8,128)(2,1)S(1)}, u32[]{:S(2)}, u32[]{:S(2)}) collective-permute-start(bf16[384,384]{1,0:T(8,128)(2,1)S(1)} %collective-permute-done.10), channel_id=1, source_target_pairs={{0,1},{1,2},{2,3},{3,4},{4,5},{5,6},{6,7},{7,128},{128,129},{129,1... | collective-permute-start | bytes 884744 | tf_op jit(solution)/shard_map/ppermute | solution.py:55
  93.7 10.2 %collective-permute-start.13 = (bf16[384,384]{1,0:T(8,128)(2,1)S(1)}, bf16[384,384]{1,0:T(8,128)(2,1)S(1)}, u32[]{:S(2)}, u32[]{:S(2)}) collective-permute-start(bf16[384,384]{1,0:T(8,128)(2,1)S(1)} %collective-permute-done.11), channel_id=1, source_target_pairs={{0,135},{1,0},{2,1},{3,2},{4,3},{5,4},{6,5},{7,6},{128,7},{129,128... | collective-permute-start | bytes 884744 | tf_op jit(solution)/shard_map/ppermute | solution.py:60
  97.5 10.0 %collective-permute-start.14 = (bf16[384,384]{1,0:T(8,128)(2,1)S(1)}, bf16[384,384]{1,0:T(8,128)(2,1)S(1)}, u32[]{:S(2)}, u32[]{:S(2)}) collective-permute-start(bf16[384,384]{1,0:T(8,128)(2,1)S(1)} %collective-permute-done.12), channel_id=1, source_target_pairs={{0,1},{1,2},{2,3},{3,4},{4,5},{5,6},{6,7},{7,128},{128,129},{129,1... | collective-permute-start | bytes 884744 | tf_op jit(solution)/shard_map/ppermute | solution.py:55
  107.6 2.2 copy-start.1
  128.5 0.7 copy-start.9
  128.5 0.8 copy-start.7
  128.5 1.6 copy-start.6
  200.8 15.0 %all-to-all-start.1 = ((bf16[16,24,384]{2,1,0:T(8,128)(2,1)}), bf16[16,24,384]{2,1,0:T(8,128)(2,1)S(1)}, u32[]{:S(2)}, u32[]{:S(2)}) async-start(bf16[16,24,384]{2,1,0:T(8,128)(2,1)} %bitcast.46), calls=%async_computation.1 | async-start | bytes 589824 | tf_op jit(solution)/shard_map/all_to_all | solution.py:74
Sparse Core Ops, SparseCore 0:
  128.6 70.2 reduce-scatter.3
